TPU v7x, 32 devices: a whole 2x2x4 slice. The times are simulated.
32 devices in a mesh: row: 2 (over core), blk: 16 (over z, y, x).
Axes of the slice: x: 2, y: 2, z: 4, core: 2. Of those that a mesh axis runs over, the one named last changes fastest.
Arguments:
- state: float32 [2, 9, 5, 16, 2048], P('row', None, None, None, 'blk'), may hold values from -6 to 6
- inflow: float32 [9, 5, 2048], P(None, None, 'blk'), may hold values from -6 to 6
- blade_counts: int32 [2], replicated, may hold values from 20 to 60
- modes: int32 [1, 4], replicated, may hold values from 1 to 40
Outputs:
- advanced: float32 [2, 9, 5, 16, 2048], P('row', None, None, None, 'blk')
All inputs are finite; a program needn't handle non-finite values.
Results may differ from a plain program's by a relative error of at most 0.0001.
Values sent between devices are 32-bit elements; how exact they have to be, the bound alone decides.
A program may use at most 64 MiB of HBM per device.

v0:
```python
import functools
import math

import jax
import jax.numpy as jnp
from jax import lax
from jax.experimental import pallas as pl
from jax.experimental.pallas import tpu as pltpu
from jax.sharding import PartitionSpec as P

DIFFUSE = 0.05
FOURTH_SMOOTH = 0.03
COURANT = 0.6
FREQ_SCALE = 0.02
MESH = pl.DeviceIdType.MESH
NEAR = DIFFUSE + 4.0 * FOURTH_SMOOTH
CENTER = -4.0 * DIFFUSE - 12.0 * FOURTH_SMOOTH
HALO = 4
PAD = 8


def packing(items, layers, width):
    seg = width // (layers + 2)
    slots = width // (layers * seg) * (seg // HALO)
    return seg, -(-items // slots)


def section(src, base, rows, start, start_base, weight, rates, emit, comps, nvars):
    width = src.shape[2]

    def at(c, v, off):
        return src[c * nvars + v, base + off : base + off + rows, :]

    def opening(v):
        return start[v, start_base : start_base + rows, :]

    coef_up = (NEAR - 0.5) - 0.25 * jnp.tanh(at(0, 1, 1))
    coef_down = (NEAR + 0.5) + 0.25 * jnp.tanh(at(0, 1, -1))
    half_turn = 0.25 * jnp.tanh(at(0, 2, 0))
    coef_next = NEAR - pltpu.roll(half_turn, width - 1, 1)
    coef_prev = NEAR + pltpu.roll(half_turn, 1, 1)
    step = (weight * COURANT) / (
        1.0 + 0.5 * jnp.tanh(opening(1)) + jnp.abs(0.5 * jnp.tanh(opening(2)))
    )

    def one(c, v):
        here, up, down = at(c, v, 0), at(c, v, 1), at(c, v, -1)
        far = (
            at(c, v, 2)
            + at(c, v, -2)
            + pltpu.roll(here, width - 2, 1)
            + pltpu.roll(here, 2, 1)
        )
        total = (
            coef_up * up
            + coef_down * down
            + coef_next * pltpu.roll(here, width - 1, 1)
            + coef_prev * pltpu.roll(here, 1, 1)
            + CENTER * here
            - FOURTH_SMOOTH * far
        )
        return here, up, down, total

    def put(c, v, total):
        k = c * nvars + v
        emit(k, start[k, start_base : start_base + rows, :] + step * total)

    def per_var(v, carry):
        stress = None
        for n in range(1, comps // 2 + 1):
            real, real_up, real_down, real_total = one(2 * n - 1, v)
            imag, imag_up, imag_down, imag_total = one(2 * n, v)
            rate = rates[n - 1]
            put(2 * n - 1, v, real_total + rate * imag)
            put(2 * n, v, imag_total - rate * real)
            term = (
                at(2 * n - 1, 1, 1) * real_up
                + at(2 * n, 1, 1) * imag_up
                - at(2 * n - 1, 1, -1) * real_down
                - at(2 * n, 1, -1) * imag_down
            )
            stress = term if stress is None else stress + term
        _, _, _, total = one(0, v)
        put(0, v, total - 0.25 * stress)
        return carry

    lax.fori_loop(0, nvars, per_var, 0, unroll=True)


def kernel(
    rows_total,
    blocks,
    nvars,
    modes_in,
    counts_in,
    state,
    inflow,
    out,
    e_main,
    e_edge,
    f_main,
    f_edge,
    x_main,
    y_main,
    in_main,
    in_edge,
    pack,
    corner,
    halo,
    low,
    high,
    low_halo,
    high_halo,
    modes,
    counts,
    local_sem,
    send_sem,
    recv_sem,
):
    fields, depth, width = state.shape
    comps = fields // nvars
    harmonics = comps // 2
    layers = depth // 8
    seg, groups = packing(fields + comps, layers, width)
    per = seg // HALO
    slots = width // (layers * seg) * per
    total_columns = width * blocks
    row = lax.axis_index("row")
    blk = lax.axis_index("blk")
    right = lax.rem(blk + 1, blocks)
    left = lax.rem(blk + blocks - 1, blocks)
    has_low = row > 0
    has_high = row < rows_total - 1

    barrier = pltpu.get_barrier_semaphore()

    def greet(r, b):
        pl.semaphore_signal(barrier, inc=1, device_id={"row": r, "blk": b}, device_id_type=MESH)

    greet(row, right)
    greet(row, left)

    @pl.when(has_high)
    def _():
        greet(row + 1, right)
        greet(row + 1, left)
        greet(row + 1, blk)

    @pl.when(has_low)
    def _():
        greet(row - 1, right)
        greet(row - 1, left)
        greet(row - 1, blk)

    fetch = pltpu.make_async_copy(state, e_main.at[:, PAD : PAD + depth, :], local_sem.at[0])
    fetch_in = pltpu.make_async_copy(inflow, in_main, local_sem.at[1])
    fetch_modes = pltpu.make_async_copy(modes_in, modes, local_sem.at[2])
    fetch_counts = pltpu.make_async_copy(counts_in, counts, local_sem.at[3])
    for copy in (fetch, fetch_in, fetch_modes, fetch_counts):
        copy.start()

    shape = (8, width)
    sub = lax.broadcasted_iota(jnp.int32, shape, 0)
    lane = lax.broadcasted_iota(jnp.int32, shape, 1)
    part, off = lane // seg, lane % seg
    fetch.wait()
    fetch_in.wait()

    def shifted(value, by):
        return pltpu.roll(value, by % width, 1)

    def spot_of(item):
        g, m = item // slots, item % slots
        return g, (m % per) * HALO + (m // per) * layers * seg

    for g in range(groups):
        edges = [jnp.zeros(shape, jnp.float32), jnp.zeros(shape, jnp.float32)]
        for k in range(g * slots, min((g + 1) * slots, fields)):
            _, p = spot_of(k)
            for layer in range(layers):
                q = p + layer * seg
                value = e_main[k, PAD + 8 * layer : PAD + 8 * layer + 8, :]
                spot = lane // HALO == q // HALO
                edges[0] = jnp.where(spot, shifted(value, q), edges[0])
                edges[1] = jnp.where(spot, shifted(value, q + HALO), edges[1])
        pack[0, g] = edges[0]
        pack[1, g] = edges[1]
    lane_in = lax.broadcasted_iota(jnp.int32, (nvars, width), 1)
    for c in range(comps):
        g, p = spot_of(fields + c)
        spot = lane_in // HALO == p // HALO
        value = in_main[c]
        pack[0, g, 0:nvars, :] = jnp.where(spot, shifted(value, p), pack[0, g, 0:nvars, :])
        pack[1, g, 0:nvars, :] = jnp.where(spot, shifted(value, p + HALO), pack[1, g, 0:nvars, :])
    for side in range(2):
        for g in range(groups):
            corner[0, side, 2 * g : 2 * g + 2, :] = pack[side, g, 0:2, :]
            corner[1, side, 2 * g : 2 * g + 2, :] = pack[side, g, 6:8, :]

    greeters = 2 + 3 * has_low.astype(jnp.int32) + 3 * has_high.astype(jnp.int32)
    pl.semaphore_wait(barrier, greeters)

    def send(src, dst, index, r, b):
        return pltpu.make_async_remote_copy(
            src_ref=src,
            dst_ref=dst,
            send_sem=send_sem.at[index],
            recv_sem=recv_sem.at[index],
            device_id={"row": r, "blk": b},
            device_id_type=MESH,
        )

    level = [send(pack.at[1], halo.at[0], 0, row, right), send(pack.at[0], halo.at[1], 1, row, left)]
    up = [
        send(corner.at[1, 1], low_halo.at[0], 2, row + 1, right),
        send(corner.at[1, 0], low_halo.at[1], 3, row + 1, left),
        send(state.at[:, pl.ds(depth - 8, 8), :], low, 4, row + 1, blk),
    ]
    down = [
        send(corner.at[0, 1], high_halo.at[0], 5, row - 1, right),
        send(corner.at[0, 0], high_halo.at[1], 6, row - 1, left),
        send(state.at[:, pl.ds(0, 8), :], high, 7, row - 1, blk),
    ]
    for copy in level:
        copy.start()

    @pl.when(has_high)
    def _():
        for copy in up:
            copy.start()

    @pl.when(has_low)
    def _():
        for copy in down:
            copy.start()

    def place(value, where_to):
        at_off = lax.broadcasted_iota(jnp.int32, value.shape, 1) % seg
        start = where_to * seg
        return jnp.where(
            at_off < 3 * HALO,
            shifted(value, start + HALO),
            shifted(value, start + 5 * HALO - width),
        )

    for k in range(fields):
        value = jnp.zeros(shape, jnp.float32)
        for layer in range(layers):
            plane = e_main[k, PAD + 8 * layer : PAD + 8 * layer + 8, :]
            value = jnp.where(part == layer + 1, place(plane, layer + 1), value)
        e_edge[k, 2:10, :] = value
    for c in range(comps):
        in_edge[c] = place(in_main[c], 1)

    fetch_modes.wait()
    fetch_counts.wait()
    sign = jnp.where((sub // 2) % 2 == 0, 1.0, -1.0).astype(jnp.float32)

    def mode_of(interface, n):
        value = jnp.int32(0)
        for i in range(rows_total - 1):
            value = value + jnp.where(interface == i, modes[i, n], 0)
        return value

    def count_of(wanted):
        value = jnp.int32(0)
        for i in range(rows_total):
            value = value + jnp.where(wanted == i, counts[i], 0)
        return value.astype(jnp.float32)

    def tables(modes_at, columns):
        made = []
        for n in range(harmonics):
            product = modes_at(n) * columns
            if total_columns & (total_columns - 1) == 0:
                turns = product & (total_columns - 1)
            else:
                turns = jnp.remainder(product, total_columns)
            angle = (2.0 * math.pi / total_columns) * turns.astype(jnp.float32)
            made.append((jnp.cos(angle), jnp.sin(angle)))
        return made

    tab_main = [
        (cosine, sign * sine)
        for cosine, sine in tables(
            lambda n: jnp.where(sub < 4, mode_of(row - 1, n), mode_of(row, n)), blk * width + lane
        )
    ]
    edge_column = jnp.where(off < 3 * HALO, off - HALO, off + width - 5 * HALO)

    def edge_mode(n):
        lower, upper = mode_of(row - 1, n), mode_of(row, n)
        rising = jnp.where(part == 0, lower, jnp.where(part == layers, upper, 0))
        falling = jnp.where(part == 1, -lower, jnp.where(part == layers + 1, -upper, 0))
        return jnp.where(sub < 4, falling, rising)

    tab_edge = tables(edge_mode, blk * width + edge_column)
    own_rate = FREQ_SCALE * count_of(row)
    next_rate = jnp.where(sub < 4, FREQ_SCALE * count_of(row - 1), FREQ_SCALE * count_of(row + 1))
    own_rates = [own_rate * float(n) for n in range(1, harmonics + 1)]
    edge_rate = jnp.where(
        part == 0,
        FREQ_SCALE * count_of(row - 1),
        jnp.where(part == layers + 1, FREQ_SCALE * count_of(row + 1), own_rate),
    )
    edge_rates = [edge_rate * float(n) for n in range(1, harmonics + 1)]
    next_rates = [next_rate * float(n) for n in range(1, harmonics + 1)]

    @pl.when(has_low)
    def _():
        up[2].wait_recv()
        x_main[:, 0:4, :] = low[:, 4:8, :]
        for k in range(fields):
            e_edge[k, 2:10, :] = jnp.where(part == 0, place(low[k], 0), e_edge[k, 2:10, :])

    @pl.when(jnp.logical_not(has_low))
    def _():
        x_main[:, 0:4, :] = jnp.zeros((fields, 4, width), jnp.float32)

    @pl.when(has_high)
    def _():
        down[2].wait_recv()
        x_main[:, 8:12, :] = high[:, 0:4, :]
        for k in range(fields):
            e_edge[k, 2:10, :] = jnp.where(
                part == layers + 1, place(high[k], layers + 1), e_edge[k, 2:10, :]
            )

    @pl.when(jnp.logical_not(has_high))
    def _():
        x_main[:, 8:12, :] = jnp.zeros((fields, 4, width), jnp.float32)

    def ends(field, inflow_of):
        @pl.when(jnp.logical_not(has_low))
        def _():
            for c in range(comps):
                for v in range(nvars):
                    plane = inflow_of[c, v : v + 1, :]
                    field[c * nvars + v, PAD - 2 : PAD, :] = jnp.broadcast_to(plane, (2, width))

        @pl.when(jnp.logical_not(has_high))
        def _():
            for k in range(fields):
                plane = field[k, PAD + depth - 1 : PAD + depth, :]
                field[k, PAD + depth : PAD + depth + 2, :] = jnp.broadcast_to(plane, (2, width))

    def turn(load, save, table):
        def per_var(v, carry):
            save(v, load(v))
            for n in range(harmonics):
                cosine, sine = table[n]
                real_at, imag_at = (2 * n + 1) * nvars + v, (2 * n + 2) * nvars + v
                real, imag = load(real_at), load(imag_at)
                save(real_at, real * cosine - imag * sine)
                save(imag_at, real * sine + imag * cosine)
            return carry

        lax.fori_loop(0, nvars, per_var, 0, unroll=True)

    def both(e, f, x, y, inflow_of, table, emit):
        x[:, 4:6, :] = e[:, PAD : PAD + 2, :]
        x[:, 6:8, :] = e[:, PAD + depth - 2 : PAD + depth, :]

        def save_first(k, value):
            e[k, PAD - 2 : PAD, :] = value[0:2]
            x[k, 4:8, :] = value[2:6]
            e[k, PAD + depth : PAD + depth + 2, :] = value[6:8]

        turn(lambda k: x[k, 2:10, :], save_first, table)
        ends(e, inflow_of)

        def keep_y(k, value):
            y[k] = value

        def keep_f(k, value):
            f[k, PAD : PAD + depth, :] = value

        section(x, 2, 8, x, 2, 0.5, next_rates, keep_y, comps, nvars)
        section(e, PAD, depth, e, PAD, 0.5, own_rates, keep_f, comps, nvars)

        def save_second(k, value):
            f[k, PAD - 2 : PAD, :] = value[0:2]
            f[k, PAD + depth : PAD + depth + 2, :] = value[6:8]

        turn(lambda k: y[k], save_second, table)
        ends(f, inflow_of)
        section(f, PAD, depth, e, PAD, 1.0, own_rates, emit, comps, nvars)

    def emit_main(k, value):
        out[k] = value

    both(e_main, f_main, x_main, y_main, in_main, tab_main, emit_main)

    for copy in level:
        copy.wait_recv()

    def beyond(value, from_left, from_right, p, start, first, last):
        at_lane = lax.broadcasted_iota(jnp.int32, value.shape, 1)
        at_part, at_off = at_lane // seg, at_lane % seg
        here = jnp.logical_and(at_part >= first, at_part <= last)
        in_left = jnp.logical_and(here, at_off < HALO)
        in_right = jnp.logical_and(here, at_off >= 5 * HALO)
        left_part = shifted(from_left, start - p)
        right_part = shifted(from_right, start + 5 * HALO - p)
        return jnp.where(in_left, left_part, jnp.where(in_right, right_part, value))

    for k in range(fields):
        g, p = spot_of(k)
        e_edge[k, 2:10, :] = beyond(
            e_edge[k, 2:10, :], halo[0, g], halo[1, g], p, seg, 1, layers
        )

    @pl.when(has_low)
    def _():
        up[0].wait_recv()
        up[1].wait_recv()
        for k in range(fields):
            g, p = spot_of(k)
            spot = slice(2 * g, 2 * g + 2)
            e_edge[k, 8:10, :] = beyond(
                e_edge[k, 8:10, :],
                low_halo[0, spot, :],
                low_halo[1, spot, :],
                p + (layers - 1) * seg,
                0,
                0,
                0,
            )

    @pl.when(jnp.logical_not(has_low))
    def _():
        for c in range(comps):
            g, p = spot_of(fields + c)
            in_edge[c] = beyond(
                in_edge[c], halo[0, g, 0:nvars, :], halo[1, g, 0:nvars, :], p, seg, 1, 1
            )

    @pl.when(has_high)
    def _():
        down[0].wait_recv()
        down[1].wait_recv()
        for k in range(fields):
            g, p = spot_of(k)
            spot = slice(2 * g, 2 * g + 2)
            e_edge[k, 2:4, :] = beyond(
                e_edge[k, 2:4, :],
                high_halo[0, spot, :],
                high_halo[1, spot, :],
                p,
                (layers + 1) * seg,
                layers + 1,
                layers + 1,
            )

    def link(field):
        def save(k, value):
            field[k, 0:2, :] = shifted(value, seg)[6:8]
            field[k, 10:12, :] = shifted(value, -seg)[0:2]

        turn(lambda k: field[k, 2:10, :], save, tab_edge)
        two = lax.broadcasted_iota(jnp.int32, (2, width), 1) // seg

        @pl.when(jnp.logical_not(has_low))
        def _():
            for c in range(comps):
                for v in range(nvars):
                    k = c * nvars + v
                    plane = jnp.broadcast_to(in_edge[c, v : v + 1, :], (2, width))
                    field[k, 0:2, :] = jnp.where(two == 1, plane, field[k, 0:2, :])

        @pl.when(jnp.logical_not(has_high))
        def _():
            for k in range(fields):
                plane = jnp.broadcast_to(field[k, 9:10, :], (2, width))
                field[k, 10:12, :] = jnp.where(two == layers, plane, field[k, 10:12, :])

    def keep_edge(k, value):
        f_edge[k, 2:10, :] = value

    def emit_edge(k, value):
        first = lane < HALO
        last = lane >= width - HALO
        outer = jnp.logical_or(first, last)
        for layer in range(layers):
            start = (layer + 1) * seg + HALO
            moved = jnp.where(
                first, shifted(value, -start), shifted(value, width - 4 * HALO - start)
            )
            rows = slice(8 * layer, 8 * layer + 8)
            out[k, rows, :] = jnp.where(outer, moved, out[k, rows, :])

    link(e_edge)
    section(e_edge, 2, 8, e_edge, 2, 0.5, edge_rates, keep_edge, comps, nvars)
    link(f_edge)
    section(f_edge, 2, 8, e_edge, 2, 1.0, edge_rates, emit_edge, comps, nvars)

    for copy in level:
        copy.wait_send()

    @pl.when(has_high)
    def _():
        for copy in up:
            copy.wait_send()

    @pl.when(has_low)
    def _():
        for copy in down:
            copy.wait_send()


def body(rows_total, blocks, state, inflow, blade_counts, modes):
    _, comps, nvars, depth, width = state.shape
    fields = comps * nvars
    _, groups = packing(fields + comps, depth // 8, width)
    corner_rows = -(-2 * groups // 8) * 8
    f32 = jnp.float32

    def buf(*shape):
        return pltpu.VMEM(shape, f32)

    tall = depth + 2 * PAD
    result = pl.pallas_call(
        functools.partial(kernel, rows_total, blocks, nvars),
        out_shape=jax.ShapeDtypeStruct((fields, depth, width), f32),
        in_specs=[
            pl.BlockSpec(memory_space=pltpu.HBM),
            pl.BlockSpec(memory_space=pltpu.HBM),
            pl.BlockSpec(memory_space=pltpu.HBM),
            pl.BlockSpec(memory_space=pltpu.HBM),
        ],
        out_specs=pl.BlockSpec(memory_space=pltpu.VMEM),
        scratch_shapes=[
            buf(fields, tall, width),
            buf(fields, 16, width),
            buf(fields, tall, width),
            buf(fields, 16, width),
            buf(fields, 16, width),
            buf(fields, 8, width),
            buf(comps, nvars, width),
            buf(comps, nvars, width),
            buf(2, groups, 8, width),
            buf(2, 2, corner_rows, width),
            buf(2, groups, 8, width),
            buf(fields, 8, width),
            buf(fields, 8, width),
            buf(2, corner_rows, width),
            buf(2, corner_rows, width),
            pltpu.SMEM(modes.shape, jnp.int32),
            pltpu.SMEM(blade_counts.shape, jnp.int32),
            pltpu.SemaphoreType.DMA((4,)),
            pltpu.SemaphoreType.DMA((8,)),
            pltpu.SemaphoreType.DMA((8,)),
        ],
        compiler_params=pltpu.CompilerParams(
            collective_id=0, has_side_effects=True, vmem_limit_bytes=16 << 20
        ),
    )(
        *(
            pltpu.with_memory_space_constraint(value, pltpu.HBM)
            for value in (modes, blade_counts, state.reshape(fields, depth, width), inflow)
        )
    )
    return result.reshape(1, comps, nvars, depth, width)


def solution(mesh):
    placed = (P("row", None, None, None, "blk"), P(None, None, "blk"), P(), P())
    return jax.shard_map(
        functools.partial(body, mesh.shape["row"], mesh.shape["blk"]),
        mesh=mesh,
        in_specs=placed,
        out_specs=P("row", None, None, None, "blk"),
        check_vma=False,
    )
```

profile of v0, /device:TPU:0, one launch (start us, length us, event | category | flops | bytes accessed | tf_op | source)
XLA Modules:
  0.0 13.4 jit_solution(10411619232469804839)
XLA Ops:
  0.0 12.6 %shard_map.46 = f32[45,16,128]{2,1,0:T(8,128)S(1)} custom-call(s32[1,4]{1,0:T(1,128)} %modes_in.1, s32[2]{0:T(128)} %counts_in.1, f32[45,16,128]{2,1,0:T(8,128)} %bitcast.3, f32[9,5,128]{2,1,0:T(8,128)} %inflow.1), custom_call_target="tpu_custom_call" | custom-call | tf_op jit(solution)/shard_map/pallas_call | solution.py:522
  12.7 0.7 %copy.6 = f32[1,9,5,16,128]{4,3,2,1,0:T(8,128)} copy(f32[1,9,5,16,128]{4,3,2,1,0:T(8,128)S(1)} %bitcast.2) | data formatting | bytes 737280
where the time goes:
time: 13.5 us; the launch traced here: 13.4 us
  Pallas kernels  12.6 us (93%)
  local copies, waits for them, and re-layouts  0.74 us (5%)
    pallas_call x1, Pallas kernels, body(): pl.pallas_call(functools.partial(kernel, rows_total, blocks, nvars), out_...  12.6 us
    unnamed x1, local copies, waits for them, and re-layouts  0.74 us

commit v1 on v0

--- a/solution.py
+++ b/solution.py
@@ -17,6 +17,8 @@
 CENTER = -4.0 * DIFFUSE - 12.0 * FOURTH_SMOOTH
 HALO = 4
 PAD = 8
+BATCH = 6
+PIECES = 3
 
 
 def packing(items, layers, width):
@@ -152,20 +154,27 @@
         greet(row - 1, left)
         greet(row - 1, blk)
 
-    fetch = pltpu.make_async_copy(state, e_main.at[:, PAD : PAD + depth, :], local_sem.at[0])
-    fetch_in = pltpu.make_async_copy(inflow, in_main, local_sem.at[1])
-    fetch_modes = pltpu.make_async_copy(modes_in, modes, local_sem.at[2])
-    fetch_counts = pltpu.make_async_copy(counts_in, counts, local_sem.at[3])
-    for copy in (fetch, fetch_in, fetch_modes, fetch_counts):
+    def fetch(first, last, index):
+        return pltpu.make_async_copy(
+            state.at[first:last], e_main.at[first:last, PAD : PAD + depth, :], local_sem.at[index]
+        )
+
+    bounds = [(g * slots, min((g + 1) * slots, fields)) for g in range(groups) if g * slots < fields]
+    for index, (opening, closing) in enumerate(bounds):
+        piece = -(-(closing - opening) // PIECES)
+        for first in range(opening, closing, piece):
+            fetch(first, min(first + piece, closing), index).start()
+    count = len(bounds)
+    fetch_in = pltpu.make_async_copy(inflow, in_main, local_sem.at[count])
+    fetch_modes = pltpu.make_async_copy(modes_in, modes, local_sem.at[count + 1])
+    fetch_counts = pltpu.make_async_copy(counts_in, counts, local_sem.at[count + 2])
+    for copy in (fetch_in, fetch_modes, fetch_counts):
         copy.start()
 
     shape = (8, width)
     sub = lax.broadcasted_iota(jnp.int32, shape, 0)
     lane = lax.broadcasted_iota(jnp.int32, shape, 1)
     part, off = lane // seg, lane % seg
-    fetch.wait()
-    fetch_in.wait()
-
     def shifted(value, by):
         return pltpu.roll(value, by % width, 1)
 
@@ -174,6 +183,8 @@
         return g, (m % per) * HALO + (m // per) * layers * seg
 
     for g in range(groups):
+        if g < count:
+            fetch(*bounds[g], g).wait()
         edges = [jnp.zeros(shape, jnp.float32), jnp.zeros(shape, jnp.float32)]
         for k in range(g * slots, min((g + 1) * slots, fields)):
             _, p = spot_of(k)
@@ -185,6 +196,7 @@
                 edges[1] = jnp.where(spot, shifted(value, q + HALO), edges[1])
         pack[0, g] = edges[0]
         pack[1, g] = edges[1]
+    fetch_in.wait()
     lane_in = lax.broadcasted_iota(jnp.int32, (nvars, width), 1)
     for c in range(comps):
         g, p = spot_of(fields + c)
@@ -204,7 +216,7 @@
         return pltpu.make_async_remote_copy(
             src_ref=src,
             dst_ref=dst,
-            send_sem=send_sem.at[index],
+            send_sem=send_sem.at[0],
             recv_sem=recv_sem.at[index],
             device_id={"row": r, "blk": b},
             device_id_type=MESH,
@@ -477,22 +489,30 @@
     def keep_edge(k, value):
         f_edge[k, 2:10, :] = value
 
-    def emit_edge(k, value):
+    def keep_last(k, value):
+        y_main[k] = value
+
+    def emit_edges():
         first = lane < HALO
-        last = lane >= width - HALO
-        outer = jnp.logical_or(first, last)
-        for layer in range(layers):
-            start = (layer + 1) * seg + HALO
-            moved = jnp.where(
-                first, shifted(value, -start), shifted(value, width - 4 * HALO - start)
-            )
-            rows = slice(8 * layer, 8 * layer + 8)
-            out[k, rows, :] = jnp.where(outer, moved, out[k, rows, :])
+        outer = jnp.logical_or(first, lane >= width - HALO)
+        for opening in range(0, fields, BATCH):
+            made = []
+            for k in range(opening, min(opening + BATCH, fields)):
+                value = y_main[k]
+                for layer in range(layers):
+                    start = (layer + 1) * seg + HALO
+                    moved = jnp.where(
+                        first, shifted(value, -start), shifted(value, width - 4 * HALO - start)
+                    )
+                    made.append((k, layer, moved))
+            for k, layer, moved in made:
+                pltpu.store(out.at[k, 8 * layer : 8 * layer + 8, :], moved, mask=outer)
 
     link(e_edge)
     section(e_edge, 2, 8, e_edge, 2, 0.5, edge_rates, keep_edge, comps, nvars)
     link(f_edge)
-    section(f_edge, 2, 8, e_edge, 2, 1.0, edge_rates, emit_edge, comps, nvars)
+    section(f_edge, 2, 8, e_edge, 2, 1.0, edge_rates, keep_last, comps, nvars)
+    emit_edges()
 
     for copy in level:
         copy.wait_send()
@@ -511,7 +531,8 @@
 def body(rows_total, blocks, state, inflow, blade_counts, modes):
     _, comps, nvars, depth, width = state.shape
     fields = comps * nvars
-    _, groups = packing(fields + comps, depth // 8, width)
+    seg, groups = packing(fields + comps, depth // 8, width)
+    slots = width // (depth // 8 * seg) * (seg // HALO)
     corner_rows = -(-2 * groups // 8) * 8
     f32 = jnp.float32
 
@@ -547,8 +568,8 @@
             buf(2, corner_rows, width),
             pltpu.SMEM(modes.shape, jnp.int32),
             pltpu.SMEM(blade_counts.shape, jnp.int32),
-            pltpu.SemaphoreType.DMA((4,)),
-            pltpu.SemaphoreType.DMA((8,)),
+            pltpu.SemaphoreType.DMA((-(-fields // slots) + 3,)),
+            pltpu.SemaphoreType.DMA((1,)),
             pltpu.SemaphoreType.DMA((8,)),
         ],
         compiler_params=pltpu.CompilerParams(

time: 13.5 us -> 12.5 us (0.926)
  Pallas kernels: 12.6 us -> 11.6 us
    pallas_call x1, Pallas kernels: 12.6 us -> 11.6 us  [body(): pl.pallas_call(functools.partial(kernel, rows_total, blocks, nvars), out_...]
where the time goes in v1:
time: 12.5 us; the launch traced here: 12.4 us
  Pallas kernels  11.6 us (93%)
  local copies, waits for them, and re-layouts  0.74 us (6%)
    pallas_call x1, Pallas kernels, body(): pl.pallas_call(functools.partial(kernel, rows_total, blocks, nvars), out_...  11.6 us
    unnamed x1, local copies, waits for them, and re-layouts  0.74 us

profile of v1, /device:TPU:0, one launch (start us, length us, event | category | flops | bytes accessed | tf_op | source)
XLA Modules:
  0.0 12.4 jit_solution(17819962929527863035)
XLA Ops:
  0.0 11.6 %shard_map.46 = f32[45,16,128]{2,1,0:T(8,128)S(1)} custom-call(s32[1,4]{1,0:T(1,128)} %modes_in.1, s32[2]{0:T(128)} %counts_in.1, f32[45,16,128]{2,1,0:T(8,128)} %bitcast.3, f32[9,5,128]{2,1,0:T(8,128)} %inflow.1), custom_call_target="tpu_custom_call" | custom-call | tf_op jit(solution)/shard_map/pallas_call | solution.py:543
  11.6 0.7 %copy.6 = f32[1,9,5,16,128]{4,3,2,1,0:T(8,128)} copy(f32[1,9,5,16,128]{4,3,2,1,0:T(8,128)S(1)} %bitcast.2) | data formatting | bytes 737280

commit v2 on v0

v2 whole, which is shorter than its diff:
```python
import functools
import math

import jax
import jax.numpy as jnp
from jax import lax
from jax.experimental import pallas as pl
from jax.experimental.pallas import tpu as pltpu
from jax.sharding import PartitionSpec as P

DIFFUSE = 0.05
FOURTH_SMOOTH = 0.03
COURANT = 0.6
FREQ_SCALE = 0.02
MESH = pl.DeviceIdType.MESH
NEAR = DIFFUSE + 4.0 * FOURTH_SMOOTH
CENTER = -4.0 * DIFFUSE - 12.0 * FOURTH_SMOOTH
HALO = 4
PAD = 8
PIECES = 5
CHUNKS = 1


def packing(comps, nvars, layers, width):
    seg = width // (comps - 1)
    per = seg // HALO
    return seg, per, -(-layers * (nvars + 1) // per)


def shifted(value, by):
    by = by % value.shape[1]
    return value if by == 0 else pltpu.roll(value, by, 1)


def section(src, base, rows, start, start_base, weight, rates, emit, comps, nvars):
    def at(c, v, off):
        return src[c * nvars + v, base + off : base + off + rows, :]

    def opening(v):
        return start[v, start_base : start_base + rows, :]

    coef_up = (NEAR - 0.5) - 0.25 * jnp.tanh(at(0, 1, 1))
    coef_down = (NEAR + 0.5) + 0.25 * jnp.tanh(at(0, 1, -1))
    half_turn = 0.25 * jnp.tanh(at(0, 2, 0))
    coef_next = NEAR - shifted(half_turn, -1)
    coef_prev = NEAR + shifted(half_turn, 1)
    step = (weight * COURANT) / (
        1.0 + 0.5 * jnp.tanh(opening(1)) + jnp.abs(0.5 * jnp.tanh(opening(2)))
    )

    def one(c, v):
        here, up, down = at(c, v, 0), at(c, v, 1), at(c, v, -1)
        far = at(c, v, 2) + at(c, v, -2) + shifted(here, -2) + shifted(here, 2)
        total = (
            coef_up * up
            + coef_down * down
            + coef_next * shifted(here, -1)
            + coef_prev * shifted(here, 1)
            + CENTER * here
            - FOURTH_SMOOTH * far
        )
        return here, up, down, total

    def put(c, v, total):
        k = c * nvars + v
        emit(k, start[k, start_base : start_base + rows, :] + step * total)

    def per_var(v, carry):
        stress = None
        for n in range(1, comps // 2 + 1):
            real, real_up, real_down, real_total = one(2 * n - 1, v)
            imag, imag_up, imag_down, imag_total = one(2 * n, v)
            rate = rates[n - 1]
            put(2 * n - 1, v, real_total + rate * imag)
            put(2 * n, v, imag_total - rate * real)
            term = (
                at(2 * n - 1, 1, 1) * real_up
                + at(2 * n, 1, 1) * imag_up
                - at(2 * n - 1, 1, -1) * real_down
                - at(2 * n, 1, -1) * imag_down
            )
            stress = term if stress is None else stress + term
        _, _, _, total = one(0, v)
        put(0, v, total - 0.25 * stress)
        return carry

    lax.fori_loop(0, nvars, per_var, 0, unroll=True)


def strip_sections(works, nvars, seg):
    def lanes(work):
        return lax.broadcasted_iota(jnp.int32, (work["rows"], work["src"].shape[2]), 1)

    def at(work, g, off):
        first = work["base"] + off
        return work["src"][g, first : first + work["rows"], :]

    def opening(work, g):
        return work["start"][g, work["first"] : work["first"] + work["rows"], :]

    def spread(work, value, v, by=0):
        near = jnp.clip(lanes(work) % seg + by, 0, seg - 1)
        return jnp.take_along_axis(value, near + seg * v, axis=1)

    coefs = []
    for work in works:
        up = spread(work, at(work, nvars, 1), 1)
        down = spread(work, at(work, nvars, -1), 1)
        after = spread(work, at(work, nvars, 0), 2, 1)
        before = spread(work, at(work, nvars, 0), 2, -1)
        if work["step"] is None:
            axial = spread(work, opening(work, nvars), 1)
            turn = spread(work, opening(work, nvars), 2)
        else:
            axial = turn = None
        coefs.append((up, down, after, before, axial, turn))
    coefs = [
        (
            (NEAR - 0.5) - 0.25 * jnp.tanh(up),
            (NEAR + 0.5) + 0.25 * jnp.tanh(down),
            NEAR - 0.25 * jnp.tanh(after),
            NEAR + 0.25 * jnp.tanh(before),
            2.0 * work["step"]
            if axial is None
            else (0.5 * COURANT)
            / (1.0 + 0.5 * jnp.tanh(axial) + jnp.abs(0.5 * jnp.tanh(turn))),
        )
        for work, (up, down, after, before, axial, turn) in zip(works, coefs)
    ]
    stresses = []
    for work in works:
        one_up, one_down = at(work, 1, 1), at(work, 1, -1)
        terms = [one_up * at(work, v, 1) - one_down * at(work, v, -1) for v in range(nvars)]
        by = seg
        while by < work["src"].shape[2]:
            odd = (lanes(work) // by) % 2 == 1
            merged = []
            for i in range(0, len(terms), 2):
                a = terms[i]
                if i + 1 < len(terms):
                    b = terms[i + 1]
                    merged.append(jnp.where(odd, b, a) + shifted(jnp.where(odd, a, b), by))
                else:
                    merged.append(a + shifted(a, by))
            terms, by = merged, 2 * by
        stresses.append(terms[0])
    for g in range(nvars + 1):
        for work, stress, (coef_up, coef_down, coef_next, coef_prev, step) in zip(
            works, stresses, coefs
        ):
            here = at(work, g, 0)
            far = at(work, g, 2) + at(work, g, -2) + shifted(here, -2) + shifted(here, 2)
            total = (
                coef_up * at(work, g, 1)
                + coef_down * at(work, g, -1)
                + coef_next * shifted(here, -1)
                + coef_prev * shifted(here, 1)
                + CENTER * here
                - FOURTH_SMOOTH * far
            )
            if g == nvars:
                total = total - 0.25 * stress
            else:
                total = total + work["rate"] * shifted(here, here.shape[1] // 2)
            work["emit"](g, opening(work, g) + step * total)
    return [each[4] for each in coefs]


def kernel(
    rows_total,
    blocks,
    modes_in,
    counts_in,
    state,
    inflow,
    out,
    e_main,
    f_main,
    x_main,
    y_main,
    in_main,
    window,
    in_window,
    pack,
    corner,
    first_planes,
    last_planes,
    halo,
    low_halo,
    high_halo,
    low,
    high,
    low_window,
    high_window,
    e_side,
    f_side,
    x_side,
    y_side,
    result,
    modes,
    counts,
    local_sem,
    send_sem,
    recv_sem,
):
    fields, depth, width = state.shape
    comps, nvars, _ = inflow.shape
    harmonics = comps // 2
    layers = depth // 8
    seg, per, wires = packing(comps, nvars, layers, width)
    total_columns = width * blocks
    row = lax.axis_index("row")
    blk = lax.axis_index("blk")
    right = lax.rem(blk + 1, blocks)
    left = lax.rem(blk + blocks - 1, blocks)
    has_low = row > 0
    has_high = row < rows_total - 1

    barrier = pltpu.get_barrier_semaphore()

    def greet(r, b):
        pl.semaphore_signal(barrier, inc=1, device_id={"row": r, "blk": b}, device_id_type=MESH)

    greet(row, right)
    greet(row, left)

    @pl.when(has_high)
    def _():
        greet(row + 1, right)
        greet(row + 1, left)
        greet(row + 1, blk)

    @pl.when(has_low)
    def _():
        greet(row - 1, right)
        greet(row - 1, left)
        greet(row - 1, blk)

    def fetch(first, last, index):
        return pltpu.make_async_copy(
            state.at[first:last], e_main.at[first:last, PAD : PAD + depth, :], local_sem.at[index]
        )

    fetch_in = pltpu.make_async_copy(inflow, in_main, local_sem.at[CHUNKS])
    fetch_modes = pltpu.make_async_copy(modes_in, modes, local_sem.at[CHUNKS + 1])
    fetch_counts = pltpu.make_async_copy(counts_in, counts, local_sem.at[CHUNKS + 2])
    fetch_in.start()
    cuts = [comps * i // CHUNKS * nvars for i in range(CHUNKS + 1)]
    bounds = list(zip(cuts, cuts[1:]))
    for index, (opening, closing) in enumerate(bounds):
        for first in range(opening, closing, PIECES):
            fetch(first, min(first + PIECES, closing), index).start()
    fetch_modes.start()
    fetch_counts.start()

    shape = (8, width)
    sub = lax.broadcasted_iota(jnp.int32, shape, 0)
    lane = lax.broadcasted_iota(jnp.int32, shape, 1)
    part, near = lane // seg, lane % seg
    slot = near // HALO

    def seat(c, v):
        if c == 0:
            return nvars, v
        return v, (c - 1) // 2 + (0 if c % 2 else harmonics)

    fetch_in.wait()
    opened = None
    for c in range(1, comps):
        _, s = seat(c, 0)
        tile = shifted(in_main[c], seg * s + 2 * HALO)
        opened = tile if opened is None else jnp.where(part[0:nvars] == s, tile, opened)
    mean = None
    for v in range(nvars):
        tile = shifted(in_main[0, v : v + 1, :], seg * v + 2 * HALO)
        mean = tile if mean is None else jnp.where(part[0:1] == v, tile, mean)
    in_window[0:nvars, :] = opened
    in_window[nvars : nvars + 1, :] = mean
    for side in range(2):
        pack[side, wires, 0:nvars, :] = shifted(opened, -HALO * (2 - side))
        pack[side, wires, nvars : nvars + 1, :] = shifted(mean, -HALO * (2 - side))

    made = {}
    for index, (opening, closing) in enumerate(bounds):
        fetch(opening, closing, index).wait()
        for k in range(opening, closing):
            first_planes[k] = e_main[k, PAD : PAD + 4, :]
            last_planes[k] = e_main[k, PAD + depth - 4 : PAD + depth, :]
            g, s = seat(*divmod(k, nvars))
            for layer in range(layers):
                tile = shifted(
                    e_main[k, PAD + 8 * layer : PAD + 8 * layer + 8, :], seg * s + 2 * HALO
                )
                old = made.get((g, layer))
                made[g, layer] = tile if old is None else jnp.where(part == s, tile, old)
    targets = [(g, layer) for g in range(nvars + 1) for layer in range(layers)]
    for side in range(2):
        for wire in range(wires):
            value = None
            for i, target in enumerate(targets[wire * per : (wire + 1) * per]):
                moved = shifted(made[target], HALO * i - HALO * (2 - side))
                value = moved if value is None else jnp.where(slot == i, moved, value)
            pack[side, wire] = value
            corner[0, side, 2 * wire : 2 * wire + 2, :] = value[0:2]
            corner[1, side, 2 * wire : 2 * wire + 2, :] = value[6:8]
    for g, layer in targets:
        window[layer, g] = made[g, layer]

    greeters = 2 + 3 * has_low.astype(jnp.int32) + 3 * has_high.astype(jnp.int32)
    pl.semaphore_wait(barrier, greeters)

    def send(src, dst, index, r, b):
        return pltpu.make_async_remote_copy(
            src_ref=src,
            dst_ref=dst,
            send_sem=send_sem.at[0],
            recv_sem=recv_sem.at[index],
            device_id={"row": r, "blk": b},
            device_id_type=MESH,
        )

    level = [send(pack.at[1], halo.at[0], 0, row, right), send(pack.at[0], halo.at[1], 1, row, left)]
    more = 0 if rows_total == 2 else 4
    up = [
        send(corner.at[1, 1], low_halo.at[0], 2, row + 1, right),
        send(corner.at[1, 0], low_halo.at[1], 3, row + 1, left),
        send(last_planes, low, 4, row + 1, blk),
        send(window.at[layers - 1], low_window, 5, row + 1, blk),
    ]
    down = [
        send(corner.at[0, 1], high_halo.at[0], 2 + more, row - 1, right),
        send(corner.at[0, 0], high_halo.at[1], 3 + more, row - 1, left),
        send(first_planes, high, 4 + more, row - 1, blk),
        send(window.at[0], high_window, 5 + more, row - 1, blk),
    ]
    for copy in level:
        copy.start()

    @pl.when(has_high)
    def _():
        for copy in up:
            copy.start()

    @pl.when(has_low)
    def _():
        for copy in down:
            copy.start()

    fetch_modes.wait()
    fetch_counts.wait()
    sign = jnp.where((sub // 2) % 2 == 0, 1.0, -1.0).astype(jnp.float32)

    def mode_of(interface, n):
        value = jnp.int32(0)
        for i in range(rows_total - 1):
            value = value + jnp.where(interface == i, modes[i, n], 0)
        return value

    def count_of(wanted):
        value = jnp.int32(0)
        for i in range(rows_total):
            value = value + jnp.where(wanted == i, counts[i], 0)
        return value.astype(jnp.float32)

    def waves(mode, columns):
        product = mode * columns
        if total_columns & (total_columns - 1) == 0:
            turns = product & (total_columns - 1)
        else:
            turns = jnp.remainder(product, total_columns)
        angle = (2.0 * math.pi / total_columns) * turns.astype(jnp.float32)
        return jnp.cos(angle), jnp.sin(angle)

    def mode_at(n):
        return jnp.where(sub < 4, mode_of(row - 1, n), mode_of(row, n))

    tab_main = []
    for n in range(harmonics):
        cosine, sine = waves(mode_at(n), blk * width + lane)
        tab_main.append((cosine, sign * sine))

    order = part % harmonics
    lane_mode = jnp.zeros(shape, jnp.int32)
    for n in range(harmonics):
        lane_mode = jnp.where(order == n, mode_at(n), lane_mode)
    flip = jnp.where(part < harmonics, -1.0, 1.0).astype(jnp.float32)
    tab_side = []
    for side in range(2):
        column = near - 2 * HALO if side == 0 else near + width - 2 * HALO
        cosine, sine = waves(lane_mode, blk * width + column)
        tab_side.append((cosine, flip * sign * sine))

    own_rate = FREQ_SCALE * count_of(row)
    next_rate = jnp.where(sub < 4, FREQ_SCALE * count_of(row - 1), FREQ_SCALE * count_of(row + 1))
    own_rates = [own_rate * float(n) for n in range(1, harmonics + 1)]
    next_rates = [next_rate * float(n) for n in range(1, harmonics + 1)]
    times = -flip * (order + 1).astype(jnp.float32)
    side_rate = jnp.concatenate([times * own_rate] * layers, axis=0)
    side_next = times * next_rate

    @pl.when(has_low)
    def _():
        for copy in up[2:]:
            copy.wait_recv()
        x_main[:, 0:4, :] = low[...]

    @pl.when(jnp.logical_not(has_low))
    def _():
        x_main[:, 0:4, :] = jnp.zeros((fields, 4, width), jnp.float32)
        low_window[...] = jnp.zeros(low_window.shape, jnp.float32)

    @pl.when(has_high)
    def _():
        for copy in down[2:]:
            copy.wait_recv()
        x_main[:, 8:12, :] = high[...]

    @pl.when(jnp.logical_not(has_high))
    def _():
        x_main[:, 8:12, :] = jnp.zeros((fields, 4, width), jnp.float32)
        high_window[...] = jnp.zeros(high_window.shape, jnp.float32)

    def last_ends(field):
        @pl.when(jnp.logical_not(has_high))
        def _():
            for k in range(field.shape[0]):
                plane = field[k, PAD + depth - 1 : PAD + depth, :]
                field[k, PAD + depth : PAD + depth + 2, :] = jnp.broadcast_to(plane, (2, width))

    def ends(field):
        @pl.when(jnp.logical_not(has_low))
        def _():
            for c in range(comps):
                for v in range(nvars):
                    plane = in_main[c, v : v + 1, :]
                    field[c * nvars + v, PAD - 2 : PAD, :] = jnp.broadcast_to(plane, (2, width))

        last_ends(field)

    def turn(load, save, table):
        def per_var(v, carry):
            save(v, load(v))
            for n in range(harmonics):
                cosine, sine = table[n]
                real_at, imag_at = (2 * n + 1) * nvars + v, (2 * n + 2) * nvars + v
                real, imag = load(real_at), load(imag_at)
                save(real_at, real * cosine - imag * sine)
                save(imag_at, real * sine + imag * cosine)
            return carry

        lax.fori_loop(0, nvars, per_var, 0, unroll=True)

    def main():
        e, f, x, y = e_main, f_main, x_main, y_main
        x[:, 4:6, :] = e[:, PAD : PAD + 2, :]
        x[:, 6:8, :] = e[:, PAD + depth - 2 : PAD + depth, :]

        def save_first(k, value):
            e[k, PAD - 2 : PAD, :] = value[0:2]
            x[k, 4:8, :] = value[2:6]
            e[k, PAD + depth : PAD + depth + 2, :] = value[6:8]

        turn(lambda k: x[k, 2:10, :], save_first, tab_main)
        ends(e)

        def keep_y(k, value):
            y[k] = value

        def keep_f(k, value):
            f[k, PAD : PAD + depth, :] = value

        section(x, 2, 8, x, 2, 0.5, next_rates, keep_y, comps, nvars)
        section(e, PAD, depth, e, PAD, 0.5, own_rates, keep_f, comps, nvars)

        def save_second(k, value):
            f[k, PAD - 2 : PAD, :] = value[0:2]
            f[k, PAD + depth : PAD + depth + 2, :] = value[6:8]

        turn(lambda k: y[k], save_second, tab_main)
        ends(f)

        def emit(k, value):
            out[k] = value

        section(f, PAD, depth, e, PAD, 1.0, own_rates, emit, comps, nvars)

    def strip(side):
        level[side].wait_recv()
        if rows_total == 2:
            up[side].wait_recv()
        else:

            @pl.when(has_low)
            def _():
                up[side].wait_recv()

            @pl.when(has_high)
            def _():
                down[side].wait_recv()

        e, f, x, y = (ref.at[side] for ref in (e_side, f_side, x_side, y_side))
        spot = HALO * (1 + side)
        here = slot == 1 + side
        cosine, sine = tab_side[side]
        for wire in range(wires):
            value = halo[side, wire]
            for i, (g, layer) in enumerate(targets[wire * per : (wire + 1) * per]):
                tile = jnp.where(here, shifted(value, spot - HALO * i), window[layer, g])
                e[g, PAD + 8 * layer : PAD + 8 * layer + 8, :] = tile
                if layer == 0:
                    x[g, 4:6, :] = tile[0:2]
                if layer == layers - 1:
                    x[g, 6:8, :] = tile[6:8]
        for g in range(nvars + 1):
            x[g, 0:2, :] = low_window[g, 4:6, :]
            x[g, 10:12, :] = high_window[g, 2:4, :]
            for layer, corners, near_window, first, to in (
                (layers - 1, low_halo, low_window, 6, 2),
                (0, high_halo, high_window, 0, 8),
            ):
                at_wire, i = divmod(g * layers + layer, per)
                pair = shifted(corners[side, 2 * at_wire : 2 * at_wire + 2, :], spot - HALO * i)
                x[g, to : to + 2, :] = jnp.where(
                    here[0:2], pair, near_window[g, first : first + 2, :]
                )

        opened = jnp.where(here, shifted(halo[side, wires], spot), in_window[...])

        def link(field, g, value, last):
            low_end = jnp.broadcast_to(opened[g : g + 1], (2, width))
            high_end = jnp.broadcast_to(last, (2, width))
            field[g, PAD - 2 : PAD, :] = jnp.where(has_low, value[0:2], low_end)
            field[g, PAD + depth : PAD + depth + 2, :] = jnp.where(has_high, value[6:8], high_end)

        def turned(g, value):
            if g == nvars:
                return value
            return value * cosine + shifted(value, width // 2) * sine

        for g in range(nvars + 1):
            value = turned(g, x[g, 2:10, :])
            x[g, 4:8, :] = value[2:6]
            link(e, g, value, e[g, PAD + depth - 1 : PAD + depth, :])

        def keep_y(g, value):
            y[g] = value

        def keep_f(g, value):
            f[g, PAD : PAD + depth, :] = value

        def work(src, base, rows, first, rate, emit, step=None):
            return dict(
                src=src,
                base=base,
                rows=rows,
                start=x if src is x else e,
                first=first,
                step=step,
                rate=rate,
                emit=emit,
            )

        near_work = work(x, 2, 8, 2, side_next, keep_y)
        own_work = work(e, PAD, depth, PAD, side_rate, keep_f)
        _, own_step = strip_sections([near_work, own_work], nvars, seg)
        for g in range(nvars + 1):
            value = turned(g, y[g])
            link(f, g, value, f[g, PAD + depth - 1 : PAD + depth, :])

        kept = {}

        def keep(g, value):
            if side == 1:
                result[g] = value
            else:
                kept[g] = value

        strip_sections([work(f, PAD, depth, PAD, side_rate, keep, own_step)], nvars, seg)
        return kept

    def emit_edges(kept):
        outer = jnp.logical_or(lane < HALO, lane >= width - HALO)
        spots = sorted((seat(*divmod(k, nvars)), k) for k in range(fields))
        for g in range(nvars + 1):
            ready = []
            for layer in range(layers):
                rows = slice(8 * layer, 8 * layer + 8)
                both = jnp.where(near < 2 * HALO, result[g, rows, :], kept[g][rows])
                for (at_g, s), k in spots:
                    if at_g == g:
                        ready.append((k, rows, shifted(both, -seg * s - 2 * HALO)))
            for k, rows, value in ready:
                pltpu.store(out.at[k, rows, :], value, mask=outer)

    main()
    strip(1)
    emit_edges(strip(0))

    for copy in level:
        copy.wait_send()

    @pl.when(has_high)
    def _():
        for copy in up:
            copy.wait_send()

    @pl.when(has_low)
    def _():
        for copy in down:
            copy.wait_send()


def body(rows_total, blocks, state, inflow, blade_counts, modes):
    _, comps, nvars, depth, width = state.shape
    fields = comps * nvars
    layers = depth // 8
    kinds = nvars + 1
    _, _, wires = packing(comps, nvars, layers, width)
    corner_rows = -(-2 * wires // 8) * 8
    f32 = jnp.float32

    def buf(*shape):
        return pltpu.VMEM(shape, f32)

    tall = depth + 2 * PAD
    result = pl.pallas_call(
        functools.partial(kernel, rows_total, blocks),
        out_shape=jax.ShapeDtypeStruct((fields, depth, width), f32),
        in_specs=[pl.BlockSpec(memory_space=pltpu.HBM)] * 4,
        out_specs=pl.BlockSpec(memory_space=pltpu.VMEM),
        scratch_shapes=[
            buf(fields, tall, width),
            buf(fields, tall, width),
            buf(fields, 16, width),
            buf(fields, 8, width),
            buf(comps, nvars, width),
            buf(layers, kinds, 8, width),
            buf(8, width),
            buf(2, wires + 1, 8, width),
            buf(2, 2, corner_rows, width),
            buf(fields, 4, width),
            buf(fields, 4, width),
            buf(2, wires + 1, 8, width),
            buf(2, corner_rows, width),
            buf(2, corner_rows, width),
            buf(fields, 4, width),
            buf(fields, 4, width),
            buf(kinds, 8, width),
            buf(kinds, 8, width),
            buf(2, kinds, tall, width),
            buf(2, kinds, tall, width),
            buf(2, kinds, 16, width),
            buf(2, kinds, 8, width),
            buf(kinds, depth, width),
            pltpu.SMEM(modes.shape, jnp.int32),
            pltpu.SMEM(blade_counts.shape, jnp.int32),
            pltpu.SemaphoreType.DMA((CHUNKS + 3,)),
            pltpu.SemaphoreType.DMA((1,)),
            pltpu.SemaphoreType.DMA((6 if rows_total == 2 else 10,)),
        ],
        compiler_params=pltpu.CompilerParams(
            collective_id=0, has_side_effects=True, vmem_limit_bytes=16 << 20
        ),
    )(
        *(
            pltpu.with_memory_space_constraint(value, pltpu.HBM)
            for value in (modes, blade_counts, state.reshape(fields, depth, width), inflow)
        )
    )
    return result.reshape(1, comps, nvars, depth, width)


def solution(mesh):
    placed = (P("row", None, None, None, "blk"), P(None, None, "blk"), P(), P())
    return jax.shard_map(
        functools.partial(body, mesh.shape["row"], mesh.shape["blk"]),
        mesh=mesh,
        in_specs=placed,
        out_specs=P("row", None, None, None, "blk"),
        check_vma=False,
    )
```

time: 13.5 us -> 11.7 us (0.87)
  Pallas kernels: 12.6 us -> 10.7 us
    pallas_call x1, Pallas kernels: 12.6 us -> 10.7 us  [body(): pl.pallas_call(functools.partial(kernel, rows_total, blocks), out_shape=j...]
where the time goes in v2:
time: 11.7 us; the launch traced here: 11.5 us
  Pallas kernels  10.7 us (91%)
  local copies, waits for them, and re-layouts  0.74 us (6%)
    pallas_call x1, Pallas kernels, body(): pl.pallas_call(functools.partial(kernel, rows_total, blocks), out_shape=j...  10.7 us
    unnamed x1, local copies, waits for them, and re-layouts  0.74 us

profile of v2, /device:TPU:0, one launch (start us, length us, event | category | flops | bytes accessed | tf_op | source)
XLA Modules:
  0.0 11.5 jit_solution(15431759602681940420)
XLA Ops:
  0.0 10.7 %shard_map.46 = f32[45,16,128]{2,1,0:T(8,128)S(1)} custom-call(s32[1,4]{1,0:T(1,128)} %modes_in.1, s32[2]{0:T(128)} %counts_in.1, f32[45,16,128]{2,1,0:T(8,128)} %bitcast.3, f32[9,5,128]{2,1,0:T(8,128)} %inflow.1), custom_call_target="tpu_custom_call" | custom-call | tf_op jit(solution)/shard_map/pallas_call | solution.py:626
  10.7 0.7 %copy.6 = f32[1,9,5,16,128]{4,3,2,1,0:T(8,128)} copy(f32[1,9,5,16,128]{4,3,2,1,0:T(8,128)S(1)} %bitcast.2) | data formatting | bytes 737280

commit v3 on v2

--- a/solution.py
+++ b/solution.py
@@ -18,7 +18,7 @@
 HALO = 4
 PAD = 8
 PIECES = 5
-CHUNKS = 1
+CHUNKS = 2
 
 
 def packing(comps, nvars, layers, width):
@@ -178,6 +178,7 @@
     f_main,
     x_main,
     y_main,
+    g_main,
     in_main,
     window,
     in_window,
@@ -294,7 +295,7 @@
                 old = made.get((g, layer))
                 made[g, layer] = tile if old is None else jnp.where(part == s, tile, old)
     targets = [(g, layer) for g in range(nvars + 1) for layer in range(layers)]
-    for side in range(2):
+    def pack_side(side):
         for wire in range(wires):
             value = None
             for i, target in enumerate(targets[wire * per : (wire + 1) * per]):
@@ -303,8 +304,33 @@
             pack[side, wire] = value
             corner[0, side, 2 * wire : 2 * wire + 2, :] = value[0:2]
             corner[1, side, 2 * wire : 2 * wire + 2, :] = value[6:8]
-    for g, layer in targets:
-        window[layer, g] = made[g, layer]
+
+    pack_side(1)
+
+    def count_of(wanted):
+        value = jnp.int32(0)
+        for i in range(rows_total):
+            value = value + jnp.where(wanted == i, counts[i], 0)
+        return value.astype(jnp.float32)
+
+    def rates_of(rate):
+        return [rate * float(n) for n in range(1, harmonics + 1)]
+
+    def inner():
+        fetch_modes.wait()
+        fetch_counts.wait()
+        own_rates = rates_of(FREQ_SCALE * count_of(row))
+        g_main[:, 2:6, :] = e_main[:, PAD : PAD + 4, :]
+        g_main[:, 6:10, :] = e_main[:, PAD + depth - 4 : PAD + depth, :]
+
+        def keep(k, value):
+            f_main[k, PAD : PAD + depth, :] = value
+
+        section(e_main, PAD, depth, e_main, PAD, 0.5, own_rates, keep, comps, nvars)
+
+    @pl.when(blk == 0)
+    def _():
+        inner()
 
     greeters = 2 + 3 * has_low.astype(jnp.int32) + 3 * has_high.astype(jnp.int32)
     pl.semaphore_wait(barrier, greeters)
@@ -333,8 +359,11 @@
         send(first_planes, high, 4 + more, row - 1, blk),
         send(window.at[0], high_window, 5 + more, row - 1, blk),
     ]
-    for copy in level:
-        copy.start()
+    level[0].start()
+    pack_side(0)
+    for g, layer in targets:
+        window[layer, g] = made[g, layer]
+    level[1].start()
 
     @pl.when(has_high)
     def _():
@@ -346,8 +375,10 @@
         for copy in down:
             copy.start()
 
-    fetch_modes.wait()
-    fetch_counts.wait()
+    @pl.when(blk != 0)
+    def _():
+        inner()
+
     sign = jnp.where((sub // 2) % 2 == 0, 1.0, -1.0).astype(jnp.float32)
 
     def mode_of(interface, n):
@@ -355,12 +386,6 @@
         for i in range(rows_total - 1):
             value = value + jnp.where(interface == i, modes[i, n], 0)
         return value
-
-    def count_of(wanted):
-        value = jnp.int32(0)
-        for i in range(rows_total):
-            value = value + jnp.where(wanted == i, counts[i], 0)
-        return value.astype(jnp.float32)
 
     def waves(mode, columns):
         product = mode * columns
@@ -390,10 +415,9 @@
         cosine, sine = waves(lane_mode, blk * width + column)
         tab_side.append((cosine, flip * sign * sine))
 
+    next_rate = jnp.where(sub < 4, FREQ_SCALE * count_of(row - 1), FREQ_SCALE * count_of(row + 1))
     own_rate = FREQ_SCALE * count_of(row)
-    next_rate = jnp.where(sub < 4, FREQ_SCALE * count_of(row - 1), FREQ_SCALE * count_of(row + 1))
-    own_rates = [own_rate * float(n) for n in range(1, harmonics + 1)]
-    next_rates = [next_rate * float(n) for n in range(1, harmonics + 1)]
+    own_rates, next_rates = rates_of(own_rate), rates_of(next_rate)
     times = -flip * (order + 1).astype(jnp.float32)
     side_rate = jnp.concatenate([times * own_rate] * layers, axis=0)
     side_next = times * next_rate
@@ -420,22 +444,21 @@
         x_main[:, 8:12, :] = jnp.zeros((fields, 4, width), jnp.float32)
         high_window[...] = jnp.zeros(high_window.shape, jnp.float32)
 
-    def last_ends(field):
-        @pl.when(jnp.logical_not(has_high))
-        def _():
-            for k in range(field.shape[0]):
-                plane = field[k, PAD + depth - 1 : PAD + depth, :]
-                field[k, PAD + depth : PAD + depth + 2, :] = jnp.broadcast_to(plane, (2, width))
-
-    def ends(field):
+    def ends(field, low_at, high_at):
         @pl.when(jnp.logical_not(has_low))
         def _():
             for c in range(comps):
                 for v in range(nvars):
                     plane = in_main[c, v : v + 1, :]
-                    field[c * nvars + v, PAD - 2 : PAD, :] = jnp.broadcast_to(plane, (2, width))
-
-        last_ends(field)
+                    field[c * nvars + v, low_at : low_at + 2, :] = jnp.broadcast_to(
+                        plane, (2, width)
+                    )
+
+        @pl.when(jnp.logical_not(has_high))
+        def _():
+            for k in range(fields):
+                plane = field[k, high_at - 1 : high_at, :]
+                field[k, high_at : high_at + 2, :] = jnp.broadcast_to(plane, (2, width))
 
     def turn(load, save, table):
         def per_var(v, carry):
@@ -451,33 +474,34 @@
         lax.fori_loop(0, nvars, per_var, 0, unroll=True)
 
     def main():
-        e, f, x, y = e_main, f_main, x_main, y_main
+        e, f, g, x, y = e_main, f_main, g_main, x_main, y_main
         x[:, 4:6, :] = e[:, PAD : PAD + 2, :]
         x[:, 6:8, :] = e[:, PAD + depth - 2 : PAD + depth, :]
 
         def save_first(k, value):
-            e[k, PAD - 2 : PAD, :] = value[0:2]
+            g[k, 0:2, :] = value[0:2]
             x[k, 4:8, :] = value[2:6]
-            e[k, PAD + depth : PAD + depth + 2, :] = value[6:8]
+            g[k, 10:12, :] = value[6:8]
 
         turn(lambda k: x[k, 2:10, :], save_first, tab_main)
-        ends(e)
+        ends(g, 0, 10)
 
         def keep_y(k, value):
             y[k] = value
 
-        def keep_f(k, value):
-            f[k, PAD : PAD + depth, :] = value
+        def keep_outer(k, value):
+            f[k, PAD : PAD + 2, :] = value[0:2]
+            f[k, PAD + depth - 2 : PAD + depth, :] = value[6:8]
 
         section(x, 2, 8, x, 2, 0.5, next_rates, keep_y, comps, nvars)
-        section(e, PAD, depth, e, PAD, 0.5, own_rates, keep_f, comps, nvars)
+        section(g, 2, 8, g, 2, 0.5, own_rates, keep_outer, comps, nvars)
 
         def save_second(k, value):
             f[k, PAD - 2 : PAD, :] = value[0:2]
             f[k, PAD + depth : PAD + depth + 2, :] = value[6:8]
 
         turn(lambda k: y[k], save_second, tab_main)
-        ends(f)
+        ends(f, PAD - 2, PAD + depth)
 
         def emit(k, value):
             out[k] = value
@@ -633,6 +657,7 @@
             buf(fields, tall, width),
             buf(fields, 16, width),
             buf(fields, 8, width),
+            buf(fields, 16, width),
             buf(comps, nvars, width),
             buf(layers, kinds, 8, width),
             buf(8, width),

time: 11.7 us -> 11.6 us (level)
  no operation moved by 1% of the time
where the time goes in v3:
time: 11.6 us; the launch traced here: 11.5 us
  Pallas kernels  10.7 us (92%)
  local copies, waits for them, and re-layouts  0.74 us (6%)
    pallas_call x1, Pallas kernels, body(): pl.pallas_call(functools.partial(kernel, rows_total, blocks), out_shape=j...  10.7 us
    unnamed x1, local copies, waits for them, and re-layouts  0.74 us

profile of v3, /device:TPU:0, one launch (start us, length us, event | category | flops | bytes accessed | tf_op | source)
XLA Modules:
  0.0 11.5 jit_solution(568256271042866959)
XLA Ops:
  0.0 10.7 %shard_map.46 = f32[45,16,128]{2,1,0:T(8,128)S(1)} custom-call(s32[1,4]{1,0:T(1,128)} %modes_in.1, s32[2]{0:T(128)} %counts_in.1, f32[45,16,128]{2,1,0:T(8,128)} %bitcast.3, f32[9,5,128]{2,1,0:T(8,128)} %inflow.1), custom_call_target="tpu_custom_call" | custom-call | tf_op jit(solution)/shard_map/pallas_call | solution.py:650
  10.7 0.7 %copy.6 = f32[1,9,5,16,128]{4,3,2,1,0:T(8,128)} copy(f32[1,9,5,16,128]{4,3,2,1,0:T(8,128)S(1)} %bitcast.2) | data formatting | bytes 737280
